TPU v7x, 256 devices: a whole 4x4x8 slice. The times are simulated.
256 devices in a mesh: row: 8 (over x, core), col: 32 (over y, z).
Axes of the slice: x: 4, y: 4, z: 8, core: 2. Of those that a mesh axis runs over, the one named last changes fastest.
Arguments:
- deflation: bfloat16 [16, 256, 16, 3072], P('row', 'col'), may hold values from 0 to 0.019897461
- coefficient: float32 [16, 256, 16], P('row', 'col'), may hold values from 1 to 10
- gradients: bfloat16 [3, 64, 64], replicated, may hold values from -0.75 to 0.75
- x_penalty: float32 [24, 256, 16], P('row', 'col'), may hold values from 1 to 10, as said below
- y_penalty: float32 [16, 288, 16], P('row', 'col'), may hold values from 1 to 10, as said below
- z_penalty: float32 [16, 256, 17], P('row', 'col'), may hold values from 1 to 10
- coarse_order: int32 [1024], replicated, may hold values from 0 to 1023, as said below
Outputs:
- coarse_blocks: float32 [1024, 7, 2304], P(('row', 'col'))
- panel: float32 [1024, 48, 528], P(('row', 'col'))
Inputs may be any that keep to these rules, and one draw needn't show every extreme that they name: `coarse_order`: each subdomain number appears once; subdomains with consecutive coarse numbers are mostly neighbours along the third or second dimension. `x_penalty`: row i * 3 + 2 equals row (i + 1) * 3: a face between two devices' blocks is held by both. `y_penalty`: column j * 9 + 8 equals column (j + 1) * 9: a face between two devices' blocks is held by both.
All inputs are finite; a program needn't handle non-finite values.
Results may differ from a plain program's by a relative error of at most 0.00044.
Values may be sent and summed in bfloat16 or wider, within the bound.
No kernel may reach another device: no remote copies, remote signals or barrier semaphores. Data moves between devices by JAX's collectives and lax.ppermute only.
A program may use at most 128 MiB of HBM per device.

v0:
```python
import jax
import jax.numpy as jnp
from jax import lax
from jax.sharding import PartitionSpec as P

NV = 48
SUB_DEV = 4
PB = 11
LINE_WEIGHTS = (1.0 / 6.0, 5.0 / 6.0, 5.0 / 6.0, 1.0 / 6.0)


def with_halo(shard, sides, width):
    for axis, dim in sides:
        size, length = (lax.axis_size(axis), shard.shape[dim])
        up = [(i, (i + 1) % size) for i in range(size - 1)]
        down = [(j, i) for i, j in up]
        last = lax.slice_in_dim(shard, length - width, length, axis=dim)
        initial = lax.slice_in_dim(shard, 0, width, axis=dim)
        before = lax.ppermute(last, axis, up)
        after = lax.ppermute(initial, axis, down)
        shard = jnp.concatenate([before, shard, after], axis=dim)
    return shard


def node_weights():
    line = jnp.array(LINE_WEIGHTS, jnp.float32)
    return (line[:, None, None] * line[None, :, None] * line[None, None, :]).reshape(64)


def contract(form, left, right):
    return jnp.einsum(form, left, right, preferred_element_type=jnp.float32)


def traces(values, axis, side):
    lead = values.ndim - 1
    nodes = values.reshape(values.shape[:lead] + (4, 4, 4, NV))
    picked = lax.index_in_dim(nodes, side, lead + axis, keepdims=False)
    return picked.reshape(values.shape[:lead] + (16, NV))


def scaled(trace, root):
    return (root[..., None, None] * trace.astype(jnp.float32)).astype(jnp.bfloat16)


def grouped(left, right, groups):
    shape = left.shape
    split = shape[:2] + (groups, shape[2] // groups) + shape[3:]
    return contract("xyskav,xyskaw->svw", left.reshape(split), right.reshape(split))


def lateral(plus, minus, root, below, above, groups):
    jump = (
        root[1:-1, :, :, None, None]
        * (plus[:-1].astype(jnp.float32) - minus[1:].astype(jnp.float32))
    ).astype(jnp.bfloat16)
    low_own = scaled(minus[0], root[0])
    low_other = scaled(below, root[0])
    high_own = scaled(plus[-1], root[-1])
    high_other = scaled(above, root[-1])
    self_part = (
        grouped(jump, jump, groups)
        + grouped(low_own[None], low_own[None], groups)
        + grouped(high_own[None], high_own[None], groups)
    )
    return (
        self_part,
        -grouped(low_own[None], low_other[None], groups),
        -grouped(high_own[None], high_other[None], groups),
    )


def vertical(plus, minus, root, groups):
    width, length, depth = plus.shape[:3]
    height = depth // groups
    plus = plus.reshape(width, length, groups, height, 16, NV)
    minus = minus.reshape(width, length, groups, height, 16, NV)
    inner_root = root[:, :, :depth].reshape(width, length, groups, height)[:, :, :, 1:]
    jump = (
        inner_root[..., None, None]
        * (plus[:, :, :, :-1].astype(jnp.float32) - minus[:, :, :, 1:].astype(jnp.float32))
    ).astype(jnp.bfloat16)
    edge_root = root[:, :, ::height]
    first = minus[:, :, :, 0]
    last = plus[:, :, :, -1]
    blank = jnp.zeros_like(last[:, :, :1])
    low_own = scaled(first, edge_root[:, :, :groups])
    low_other = scaled(jnp.concatenate([blank, last[:, :, :-1]], axis=2), edge_root[:, :, :groups])
    high_own = scaled(last, edge_root[:, :, 1:])
    high_other = scaled(jnp.concatenate([first[:, :, 1:], blank], axis=2), edge_root[:, :, 1:])
    pairing = "xysav,xysaw->svw"
    self_part = (
        contract("xyskav,xyskaw->svw", jump, jump)
        + contract(pairing, low_own, low_own)
        + contract(pairing, high_own, high_own)
    )
    return (
        self_part,
        -contract(pairing, low_own, low_other),
        -contract(pairing, high_own, high_other),
    )


def volume(values, coefficient, gradients, groups):
    width, length, depth = values.shape[:3]
    nodes = values.reshape(width, length, depth, 64, NV)
    factor = jnp.sqrt(coefficient[..., None] * node_weights())
    total = jnp.zeros((groups, NV, NV), jnp.float32)
    for axis in range(3):
        product = contract("ab,xyzbv->xyzav", gradients[axis], nodes)
        rounded = (product * factor[..., None]).astype(jnp.bfloat16)
        rounded = rounded.reshape(width, length, groups, depth // groups, 64, NV)
        total = total + contract("xyskav,xyskaw->svw", rounded, rounded)
    return total


def panel_rows(blocks, column_block, present):
    picks = (
        present[:, :, None]
        & (column_block[:, :, None] == jnp.arange(PB, dtype=jnp.int32)[None, None, :])
    ).astype(jnp.float32)
    rows = jnp.einsum("stp,stvw->svpw", picks, blocks, precision=lax.Precision.HIGHEST).reshape(
        blocks.shape[0], NV, PB * NV
    )
    select = (column_block[:, :1] == jnp.arange(PB, dtype=jnp.int32)[None, :]).astype(jnp.float32)
    share = jnp.einsum("sp,svq->pvq", select, rows, precision=lax.Precision.HIGHEST)
    return (rows, select, share)


def finish(rows, select, assembled):
    whole = assembled.reshape(PB * NV, PB * NV)
    factor = jnp.linalg.cholesky(0.5 * (whole + whole.T))
    count = rows.shape[0]
    solved = jax.scipy.linalg.solve_triangular(
        factor, rows.reshape(count * NV, PB * NV).T, lower=True
    ).T.reshape(count, NV, PB * NV)
    inside = jnp.einsum(
        "sp,pvq->svq", select, factor.reshape(PB, NV, PB * NV), precision=lax.Precision.HIGHEST
    )
    return jnp.where(jnp.sum(select, axis=1)[:, None, None] > 0, inside, solved)


def shards(deflation, coefficient, gradients, x_penalty, y_penalty, z_penalty, coarse_order):
    plus_x = traces(deflation, 0, 3)
    minus_x = traces(deflation, 0, 0)
    plus_y = traces(deflation, 1, 3)
    minus_y = traces(deflation, 1, 0)
    padded = with_halo(deflation, (("row", 0), ("col", 1)), 1)
    below_x = traces(padded[0, 1:-1], 0, 3)
    above_x = traces(padded[-1, 1:-1], 0, 0)
    below_y = traces(padded[1:-1, 0], 1, 3)
    above_y = traces(padded[1:-1, -1], 1, 0)
    x_root = jnp.sqrt(x_penalty)
    y_root = jnp.sqrt(y_penalty)
    z_root = jnp.sqrt(z_penalty)
    self_x, low_x, high_x = lateral(plus_x, minus_x, x_root, below_x, above_x, SUB_DEV)
    self_y, low_y, high_y = lateral(
        jnp.swapaxes(plus_y, 0, 1),
        jnp.swapaxes(minus_y, 0, 1),
        jnp.swapaxes(y_root, 0, 1),
        below_y,
        above_y,
        SUB_DEV,
    )
    self_z, low_z, high_z = vertical(
        traces(deflation, 2, 3), traces(deflation, 2, 0), z_root, SUB_DEV
    )
    diagonal = volume(deflation, coefficient, gradients, SUB_DEV) + self_x + self_y + self_z
    blocks = jnp.stack([diagonal, low_x, high_x, low_y, high_y, low_z, high_z], axis=1)
    row_pos = lax.axis_index("row")
    col_pos = lax.axis_index("col")
    row_count = lax.axis_size("row")
    col_count = lax.axis_size("col")
    device = row_pos * col_count + col_pos
    local = jnp.arange(SUB_DEV, dtype=jnp.int32)
    owner = device * SUB_DEV + local
    stride = col_count * SUB_DEV
    neighbours = jnp.stack(
        [
            owner,
            owner - stride,
            owner + stride,
            owner - SUB_DEV,
            owner + SUB_DEV,
            owner - 1,
            owner + 1,
        ],
        axis=1,
    )
    always = jnp.ones((SUB_DEV,), bool)
    present = jnp.stack(
        [
            always,
            always & (row_pos > 0),
            always & (row_pos < row_count - 1),
            always & (col_pos > 0),
            always & (col_pos < col_count - 1),
            local > 0,
            local < SUB_DEV - 1,
        ],
        axis=1,
    )
    match = (
        neighbours[:, :, None] == jnp.arange(coarse_order.shape[0], dtype=jnp.int32)[None, None, :]
    )
    column_block = jnp.sum(jnp.where(match, coarse_order[None, None, :], 0), axis=-1)
    rows, select, share = panel_rows(blocks, column_block, present)
    assembled = lax.psum(share, ("row", "col"))
    panel = finish(rows, select, assembled)
    return (blocks.reshape(SUB_DEV, 7, NV * NV), panel)


def solution(mesh):
    in_specs = (
        P("row", "col", None, None),
        P("row", "col", None),
        P(),
        P("row", "col", None),
        P("row", "col", None),
        P("row", "col", None),
        P(),
    )
    out_specs = (P(("row", "col"), None, None), P(("row", "col"), None, None))
    return jax.shard_map(shards, mesh=mesh, in_specs=in_specs, out_specs=out_specs, check_vma=False)
```

profile of v0, /device:TPU:6, one launch (start us, length us, event | category | flops | bytes accessed | tf_op | source)
XLA Modules:
  0.0 590.4 jit_solution(2413078286542607056)
XLA Ops:
  7.2 2.8 fusion.121
  10.0 1.9 collective-permute-start
  11.9 3.6 collective-permute-start.1
  15.6 5.4 reshape.330
  21.0 2.6 fusion.118
  23.6 2.6 convert_subtract_fusion
  26.1 4.1 fusion.119
  30.8 5.3 reshape.326
  36.5 5.3 multiply_convert_fusion
  44.0 4.5 fusion.117
  52.7 1.5 copy.257
  57.8 4.5 convolution_bitcast_fusion.12
  62.3 1.6 convolution_bitcast_fusion.13
  65.5 2.2 copy.265
  70.2 1.8 slice_bitcast_fusion.1
  73.7 1.6 copy_convert_fusion
  77.2 2.0 multiply_convert_fusion.2
  79.9 2.9 copy.249
  82.8 1.6 copy.253
  84.4 1.6 copy.245
  86.2 3.1 convolution_bitcast_fusion.1
  89.4 6.7 %reshape_squeeze.26 = bf16[8,16,4,4,4,48]{5,4,3,2,1,0:T(4,128)(2,1)} reshape(bf16[1,8,16,3072]{3,2,1,0:T(8,128)(2,1)} %collective-permute-done) | data formatting | bytes 1572864 | tf_op jit(solution)/shard_map/reshape;squeeze | solution.py:36
  100.9 6.2 %reshape_squeeze.27 = bf16[8,16,4,4,4,48]{5,4,3,2,1,0:T(4,128)(2,1)} reshape(bf16[1,8,16,3072]{3,2,1,0:T(8,128)(2,1)} %collective-permute-done.1) | data formatting | bytes 1572864 | tf_op jit(solution)/shard_map/reshape;squeeze | solution.py:36
  111.2 1.3 constant_dynamic-update-slice_fusion.2
  115.0 4.7 collective-permute-start.2
  119.7 1.5 collective-permute-start.3
  122.8 1.5 bitcast_dynamic-update-slice_fusion.7
  129.0 3.3 collective-permute-done.3
  140.9 1.6 copy.281
  145.4 259.5 %all-reduce.7.cloned.1.call-done = f32[528,528]{0,1:T(8,128)} async-done(((f32[528,528]{0,1:T(8,128)}), f32[528,528]{0,1:T(8,128)}) %all-reduce.7.cloned.1.call-update) | async-done | bytes 1115152 | tf_op jit(solution)/shard_map/psum | solution.py:207
  404.9 3.0 copy.282
  407.9 1.5 fusion.3
  411.2 11.9 %cholesky.134 = f32[128,128]{1,0:T(8,128)S(1)} custom-call(f32[128,128]{1,0:T(8,128)S(1)} %cholesky.346), custom_call_target="Cholesky" | custom-call | tf_op jit(solution)/shard_map/jit(cholesky)/cholesky | solution.py:131
  423.2 9.8 %custom-call.39 = f32[1,128,128]{1,2,0:T(8,128)S(1)} custom-call(f32[1,128,128]{2,1,0:T(8,128)S(1)} %get-tuple-element.54), custom_call_target="InvertDiagBlocksLowerTriangular" | custom-call | tf_op jit(solution)/shard_map/jit(cholesky)/cholesky | solution.py:131
  435.6 11.7 %cholesky.274 = f32[128,128]{1,0:T(8,128)S(1)} custom-call(f32[128,128]{1,0:T(8,128)S(1)} %cholesky.350), custom_call_target="Cholesky" | custom-call | tf_op jit(solution)/shard_map/jit(cholesky)/cholesky | solution.py:131
  448.7 9.8 %custom-call.40 = f32[1,128,128]{1,2,0:T(8,128)S(1)} custom-call(f32[1,128,128]{2,1,0:T(8,128)S(1)} %get-tuple-element.51), custom_call_target="InvertDiagBlocksLowerTriangular" | custom-call | tf_op jit(solution)/shard_map/jit(cholesky)/cholesky | solution.py:131
  460.1 12.1 %cholesky.295 = f32[128,128]{1,0:T(8,128)S(1)} custom-call(f32[128,128]{1,0:T(8,128)S(1)} %cholesky.355), custom_call_target="Cholesky" | custom-call | tf_op jit(solution)/shard_map/jit(cholesky)/cholesky | solution.py:131
  472.8 9.8 %custom-call.41 = f32[1,128,128]{1,2,0:T(8,128)S(1)} custom-call(f32[1,128,128]{2,1,0:T(8,128)S(1)} %get-tuple-element.48), custom_call_target="InvertDiagBlocksLowerTriangular" | custom-call | tf_op jit(solution)/shard_map/jit(cholesky)/cholesky | solution.py:131
  484.1 11.7 %cholesky.314 = f32[128,128]{1,0:T(8,128)S(1)} custom-call(f32[128,128]{1,0:T(8,128)S(1)} %cholesky.360), custom_call_target="Cholesky" | custom-call | tf_op jit(solution)/shard_map/jit(cholesky)/cholesky | solution.py:131
  496.5 9.8 %custom-call.42 = f32[1,128,128]{1,2,0:T(8,128)S(1)} custom-call(f32[1,128,128]{2,1,0:T(8,128)S(1)} %get-tuple-element.45), custom_call_target="InvertDiagBlocksLowerTriangular" | custom-call | tf_op jit(solution)/shard_map/jit(cholesky)/cholesky | solution.py:131
  507.4 1.5 cholesky.334
  514.0 11.9 %while.1 = (s32[]{:T(128)}, f32[528,528]{1,0:T(8,128)}, s32[4,2]{0,1:T(2,128)S(1)}, f32[4,128,128]{2,1,0:T(8,128)S(1)}, s32[]{:T(128)}) while((s32[]{:T(128)}, f32[528,528]{1,0:T(8,128)}, s32[4,2]{0,1:T(2,128)S(1)}, f32[4,128,128]{2,1,0:T(8,128)S(1)}, s32[]{:T(128)}) %tuple.72), condition=%wide.while_cond, body=%wide.while_body.sunk | while | flops 2 | bytes 131181 | solution.py:133
  514.8 2.3 bitcast_dynamic-update-slice_fusion.9
  517.8 2.3 bitcast_dynamic-update-slice_fusion.9
  520.7 2.3 bitcast_dynamic-update-slice_fusion.9
  523.6 2.3 bitcast_dynamic-update-slice_fusion.9
  526.0 49.1 %custom-call.43 = f32[5,128,128]{1,2,0:T(8,128)S(1)} custom-call(f32[5,128,128]{2,1,0:T(8,128)S(1)} %pad_maximum_fusion), custom_call_target="InvertDiagBlocksLowerTriangular" | custom-call | tf_op jit(solution)/shard_map/jit(_solve_triangular)/triangular_solve | solution.py:133
  578.3 1.3 convolution_subtract_fusion.4
  (284 shorter events, 70.8 us)
Async XLA Ops:
  7.2 8.4 %copy-start.3 = (bf16[2,8,16,3072]{3,2,1,0:T(8,128)(2,1)S(1)}, bf16[2,8,16,3072]{3,2,1,0:T(8,128)(2,1)}, u32[]{:S(2)}) copy-start(bf16[2,8,16,3072]{3,2,1,0:T(8,128)(2,1)} %param.8) | copy-start | bytes 4718596
  7.2 397.8 %all-reduce.7.cloned.1.call-start = ((), (), s32[]{:S(2)}) async-start(), calls=%async_computation | async-start | bytes 2703360 | tf_op jit(solution)/shard_map/psum | solution.py:207
  10.0 79.4 %collective-permute-start = (bf16[1,8,16,3072]{3,2,1,0:T(8,128)(2,1)}, bf16[1,8,16,3072]{3,2,1,0:T(8,128)(2,1)}, u32[]{:S(2)}, u32[]{:S(2)}) collective-permute-start(bf16[1,8,16,3072]{3,2,1,0:T(8,128)(2,1)} %get-tuple-element.43), channel_id=1, source_target_pairs={{0,32},{32,64},{64,96},{96,128},{128,160},{160,192},{192,224},{1,3... | collective-permute-start | bytes 2359304 | tf_op jit(solution)/shard_map/ppermute | solution.py:19
  11.9 88.9 %collective-permute-start.1 = (bf16[1,8,16,3072]{3,2,1,0:T(8,128)(2,1)}, bf16[1,8,16,3072]{3,2,1,0:T(8,128)(2,1)}, u32[]{:S(2)}, u32[]{:S(2)}) collective-permute-start(bf16[1,8,16,3072]{3,2,1,0:T(8,128)(2,1)} %get-tuple-element.42), channel_id=1, source_target_pairs={{32,0},{64,32},{96,64},{128,96},{160,128},{192,160},{224,192},{33,... | collective-permute-start | bytes 2359304 | tf_op jit(solution)/shard_map/ppermute | solution.py:20
  26.1 4.1 copy-start.40
  30.3 5.8 copy-start.36
  30.8 5.3 copy-start.45
  30.8 5.5 copy-start.41
  30.8 5.7 copy-start.35
  36.5 5.3 copy-start
  41.8 2.2 copy-start.2
  44.0 8.1 %copy-start.39 = (f32[3,8,16]{2,1,0:T(8,128)S(1)}, f32[3,8,16]{2,1,0:T(8,128)}, u32[]{:S(2)}) copy-start(f32[3,8,16]{2,1,0:T(8,128)} %param.11) | copy-start | bytes 4612
  52.1 2.1 copy-start.12
  65.1 4.1 copy-start.19
  65.5 2.2 copy-start.42
  67.7 4.3 copy-start.54
  67.7 4.3 copy-start.55
  67.7 4.3 copy-start.56
  67.7 4.3 copy-start.57
  67.7 4.3 copy-start.58
  67.7 4.3 copy-start.59
  67.7 4.3 copy-start.60
  67.7 4.3 copy-start.46
  67.7 4.7 copy-start.34
  67.7 6.0 %copy-start.17 = (bf16[1,8,16,1,4,4,48]{6,5,4,3,2,1,0:T(4,128)(2,1)S(1)}, bf16[1,8,16,1,4,4,48]{6,5,4,3,2,1,0:T(4,128)(2,1)}, u32[]{:S(2)}) copy-start(bf16[1,8,16,1,4,4,48]{6,5,4,3,2,1,0:T(4,128)(2,1)} %get-tuple-element.36) | copy-start | bytes 589828
  67.8 6.0 %copy-start.18 = (bf16[1,8,16,1,4,4,48]{6,5,4,3,2,1,0:T(4,128)(2,1)S(1)}, bf16[1,8,16,1,4,4,48]{6,5,4,3,2,1,0:T(4,128)(2,1)}, u32[]{:S(2)}) copy-start(bf16[1,8,16,1,4,4,48]{6,5,4,3,2,1,0:T(4,128)(2,1)} %get-tuple-element.37) | copy-start | bytes 589828
  67.9 2.3 copy-start.32
  70.2 5.5 copy-start.15
  70.2 5.8 copy-start.21
  72.4 3.0 copy-start.38
  72.4 3.0 copy-start.50
  73.7 3.4 copy-start.1
  79.9 2.9 copy-start.8
  112.8 8.4 %copy-start.20 = (f32[1,8,16,1,4,4,48]{6,1,5,4,2,3,0:T(8,128)S(1)}, f32[1,8,16,1,4,4,48]{6,1,5,4,2,3,0:T(8,128)}, u32[]{:S(2)}) copy-start(f32[1,8,16,1,4,4,48]{6,1,5,4,2,3,0:T(8,128)} %copy.245) | copy-start | bytes 1179652
  112.8 8.4 %copy-start.43 = (f32[1,8,16]{1,2,0:T(8,128)S(1)}, f32[1,8,16]{1,2,0:T(8,128)}, u32[]{:S(2)}) copy-start(f32[1,8,16]{1,2,0:T(8,128)} %get-tuple-element.55) | copy-start | bytes 1540
  112.8 8.4 %copy-start.64 = (f32[4,48,48]{2,1,0:T(8,128)S(1)}, f32[4,48,48]{2,1,0:T(8,128)}, u32[]{:S(2)}) copy-start(f32[4,48,48]{2,1,0:T(8,128)} %convolution_bitcast_fusion.10) | copy-start | bytes 110596
  115.0 6.7 %copy-start.28 = (f32[4,48,48]{2,1,0:T(8,128)S(1)}, f32[4,48,48]{2,1,0:T(8,128)}, u32[]{:S(2)}) copy-start(f32[4,48,48]{2,1,0:T(8,128)} %convolution_bitcast_fusion.12) | copy-start | bytes 110596
  115.0 6.7 %copy-start.29 = (f32[4,48,48]{2,1,0:T(8,128)S(1)}, f32[4,48,48]{2,1,0:T(8,128)}, u32[]{:S(2)}) copy-start(f32[4,48,48]{2,1,0:T(8,128)} %convolution_bitcast_fusion.13) | copy-start | bytes 110596
  115.0 6.7 %copy-start.33 = (f32[4,48,48]{2,1,0:T(8,128)S(1)}, f32[4,48,48]{2,1,0:T(8,128)}, u32[]{:S(2)}) copy-start(f32[4,48,48]{2,1,0:T(8,128)} %fusion.24) | copy-start | bytes 110596
  115.0 12.5 %collective-permute-start.2 = (bf16[4,1,16,3072]{3,2,1,0:T(8,128)(2,1)}, bf16[4,1,16,3072]{3,2,1,0:T(8,128)(2,1)}, u32[]{:S(2)}, u32[]{:S(2)}) collective-permute-start(bf16[4,1,16,3072]{3,2,1,0:T(8,128)(2,1)} %get-tuple-element.41), channel_id=1, source_target_pairs={{0,1},{1,2},{2,3},{3,4},{4,5},{5,6},{6,7},{7,8},{8,9},{9,10},{10,1... | collective-permute-start | bytes 1179656 | tf_op jit(solution)/shard_map/ppermute | solution.py:19
  119.7 12.6 %collective-permute-start.3 = (bf16[4,1,16,3072]{3,2,1,0:T(8,128)(2,1)}, bf16[4,1,16,3072]{3,2,1,0:T(8,128)(2,1)}, u32[]{:S(2)}, u32[]{:S(2)}) collective-permute-start(bf16[4,1,16,3072]{3,2,1,0:T(8,128)(2,1)} %get-tuple-element.40), channel_id=1, source_target_pairs={{1,0},{2,1},{3,2},{4,3},{5,4},{6,5},{7,6},{8,7},{9,8},{10,9},{11,1... | collective-permute-start | bytes 1179656 | tf_op jit(solution)/shard_map/ppermute | solution.py:20
  125.8 8.1 %copy-start.16 = (f32[1,2,16,16,48]{4,2,3,0,1:T(8,128)S(1)}, f32[1,2,16,16,48]{4,2,3,0,1:T(8,128)}, u32[]{:S(2)}) copy-start(f32[1,2,16,16,48]{4,2,3,0,1:T(8,128)} %slice_convert_fusion.1) | copy-start | bytes 294916
  129.0 5.6 slice-start
  133.8 2.0 slice-start.1
  133.9 2.0 copy-start.48
  404.9 3.0 copy-start.7
  512.7 13.2 %copy-start.31 = (f32[128,112]{1,0:T(8,128)S(1)}, f32[128,112]{1,0:T(8,128)}, u32[]{:S(2)}) copy-start(f32[128,112]{1,0:T(8,128)} %pad_convert_fusion) | copy-start | bytes 172036
  576.5 4.8 copy-start.61
  (26 other events, 34.9 us)
Sparse Core Ops, SparseCore 0:
  142.6 262.2 all-reduce.6
where the time goes:
time: 597 us; the launch traced here: 590 us
  waiting for transfers between devices  264 us (44%)
  other arithmetic  157 us (26%)
  local copies, waits for them, and re-layouts  95.1 us (16%)
  matrix products  44.6 us (7%)
  between operations  18.6 us (3%)
  starting transfers between devices  11.8 us (2%)
    psum x1, waiting for transfers between devices, shards(): assembled = lax.psum(share, ('row', 'col'))  259 us
    another operation x19, other arithmetic, finish(): factor = jnp.linalg.cholesky(0.5 * (whole + whole.T))  91.6 us
    another operation x7, other arithmetic, finish(): jax.scipy.linalg.solve_triangular(factor, rows.reshape(count * NV, PB * N...  50.7 us
    dot_general x21, matrix products, contract(): return jnp.einsum(form, left, right, preferred_element_type=jnp.float32)  28.5 us
    slice x10, local copies, waits for them, and re-layouts, traces(): picked = lax.index_in_dim(nodes, side, lead + axis, keepdims=False)  16.6 us
    another operation x4, local copies, waits for them, and re-layouts, traces(): nodes = values.reshape(values.shape[:lead] + (4, 4, 4, NV))  14 us
    unnamed x143, local copies, waits for them, and re-layouts  12.1 us
  transfers between devices with their start and end apart: 5, of which 3 were waited for; matrix products, arithmetic and copies ran while one was open for 15% of the time, Pallas kernels for 0%

commit v1 on v0

--- a/solution.py
+++ b/solution.py
@@ -204,7 +204,7 @@
     )
     column_block = jnp.sum(jnp.where(match, coarse_order[None, None, :], 0), axis=-1)
     rows, select, share = panel_rows(blocks, column_block, present)
-    assembled = lax.psum(share, ("row", "col"))
+    assembled = lax.psum(lax.psum(share, "row"), "col")
     panel = finish(rows, select, assembled)
     return (blocks.reshape(SUB_DEV, 7, NV * NV), panel)
 

time: 597 us -> 560 us (0.938)
  waiting for transfers between devices: 264 us -> 224 us
    psum x1 -> x2, waiting for transfers between devices: 259 us -> 219 us  [shards(): assembled = lax.psum(lax.psum(share, 'row'), 'col')]
    unnamed x143 -> x141, local copies, waits for them, and re-layouts: 12.1 us -> 12 us
  transfers between devices with their start and end apart: 5 -> 6, of which waited for: 3 -> 4; matrix products, arithmetic and copies ran while one was open for 15% -> 17% of each run, Pallas kernels for 0% -> 0%
where the time goes in v1:
time: 560 us; the launch traced here: 553 us
  waiting for transfers between devices  224 us (40%)
  other arithmetic  156 us (28%)
  local copies, waits for them, and re-layouts  96.2 us (17%)
  matrix products  46 us (8%)
  between operations  19 us (3%)
  starting transfers between devices  11.8 us (2%)
    psum x2, waiting for transfers between devices, shards(): assembled = lax.psum(lax.psum(share, 'row'), 'col')  219 us
    another operation x19, other arithmetic, finish(): factor = jnp.linalg.cholesky(0.5 * (whole + whole.T))  91.6 us
    another operation x7, other arithmetic, finish(): jax.scipy.linalg.solve_triangular(factor, rows.reshape(count * NV, PB * N...  51.2 us
    dot_general x21, matrix products, contract(): return jnp.einsum(form, left, right, preferred_element_type=jnp.float32)  28.6 us
    slice x10, local copies, waits for them, and re-layouts, traces(): picked = lax.index_in_dim(nodes, side, lead + axis, keepdims=False)  16.5 us
    another operation x4, local copies, waits for them, and re-layouts, traces(): nodes = values.reshape(values.shape[:lead] + (4, 4, 4, NV))  13.9 us
    another operation x13, local copies, waits for them, and re-layouts  12 us
    unnamed x141, local copies, waits for them, and re-layouts  12 us
  transfers between devices with their start and end apart: 6, of which 4 were waited for; matrix products, arithmetic and copies ran while one was open for 17% of the time, Pallas kernels for 0%

profile of v1, /device:TPU:6, one launch (start us, length us, event | category | flops | bytes accessed | tf_op | source)
XLA Modules:
  0.0 552.7 jit_solution(14297277470521270706)
XLA Ops:
  7.2 2.8 fusion.121
  10.0 1.9 collective-permute-start
  11.9 3.6 collective-permute-start.1
  15.6 5.4 reshape.330
  21.0 2.6 fusion.118
  23.6 2.6 convert_subtract_fusion
  26.1 4.1 fusion.119
  30.3 5.3 reshape.326
  36.0 5.3 multiply_convert_fusion
  43.5 4.5 fusion.117
  52.1 1.5 copy.257
  56.5 4.4 convolution_bitcast_fusion.12
  61.0 1.6 convolution_bitcast_fusion.13
  64.2 2.2 copy.265
  68.9 1.8 slice_bitcast_fusion.1
  72.4 1.6 copy_convert_fusion
  75.8 2.0 multiply_convert_fusion.2
  78.4 2.9 copy.249
  81.3 1.6 copy.253
  82.9 1.6 copy.245
  85.3 3.3 convolution_bitcast_fusion.1
  88.6 6.6 %reshape_squeeze.26 = bf16[8,16,4,4,4,48]{5,4,3,2,1,0:T(4,128)(2,1)} reshape(bf16[1,8,16,3072]{3,2,1,0:T(8,128)(2,1)} %collective-permute-done) | data formatting | bytes 1572864 | tf_op jit(solution)/shard_map/reshape;squeeze | solution.py:36
  99.4 6.2 %reshape_squeeze.27 = bf16[8,16,4,4,4,48]{5,4,3,2,1,0:T(4,128)(2,1)} reshape(bf16[1,8,16,3072]{3,2,1,0:T(8,128)(2,1)} %collective-permute-done.1) | data formatting | bytes 1572864 | tf_op jit(solution)/shard_map/reshape;squeeze | solution.py:36
  112.0 4.7 collective-permute-start.2
  126.0 3.3 collective-permute-done.3
  132.9 1.9 bitcast_dynamic-update-slice_fusion.1
  136.6 2.4 fusion.33
  140.6 68.5 %all-reduce.8.cloned.1.call-done = f32[11,48,528]{2,0,1:T(8,128)} async-done(((f32[11,48,528]{2,0,1:T(8,128)}), f32[11,48,528]{2,0,1:T(8,128)}) %all-reduce.8.cloned.1.call-update) | async-done | bytes 1115152 | tf_op jit(solution)/shard_map/psum | solution.py:207
  209.1 2.0 copy.280
  211.1 1.6 copy.281
  216.0 150.6 %all-reduce.10.cloned.1.call-done = f32[528,528]{0,1:T(8,128)} async-done(((f32[528,528]{0,1:T(8,128)}), f32[528,528]{0,1:T(8,128)}) %all-reduce.10.cloned.1.call-update) | async-done | bytes 1115152 | tf_op jit(solution)/shard_map/psum | solution.py:207
  366.6 3.0 copy.282
  369.6 1.5 fusion.3
  372.9 11.7 %cholesky.134 = f32[128,128]{1,0:T(8,128)S(1)} custom-call(f32[128,128]{1,0:T(8,128)S(1)} %cholesky.346), custom_call_target="Cholesky" | custom-call | tf_op jit(solution)/shard_map/jit(cholesky)/cholesky | solution.py:131
  384.7 9.8 %custom-call.39 = f32[1,128,128]{1,2,0:T(8,128)S(1)} custom-call(f32[1,128,128]{2,1,0:T(8,128)S(1)} %get-tuple-element.54), custom_call_target="InvertDiagBlocksLowerTriangular" | custom-call | tf_op jit(solution)/shard_map/jit(cholesky)/cholesky | solution.py:131
  397.1 11.9 %cholesky.274 = f32[128,128]{1,0:T(8,128)S(1)} custom-call(f32[128,128]{1,0:T(8,128)S(1)} %cholesky.350), custom_call_target="Cholesky" | custom-call | tf_op jit(solution)/shard_map/jit(cholesky)/cholesky | solution.py:131
  410.4 9.8 %custom-call.40 = f32[1,128,128]{1,2,0:T(8,128)S(1)} custom-call(f32[1,128,128]{2,1,0:T(8,128)S(1)} %get-tuple-element.51), custom_call_target="InvertDiagBlocksLowerTriangular" | custom-call | tf_op jit(solution)/shard_map/jit(cholesky)/cholesky | solution.py:131
  421.8 11.7 %cholesky.295 = f32[128,128]{1,0:T(8,128)S(1)} custom-call(f32[128,128]{1,0:T(8,128)S(1)} %cholesky.355), custom_call_target="Cholesky" | custom-call | tf_op jit(solution)/shard_map/jit(cholesky)/cholesky | solution.py:131
  434.2 9.8 %custom-call.41 = f32[1,128,128]{1,2,0:T(8,128)S(1)} custom-call(f32[1,128,128]{2,1,0:T(8,128)S(1)} %get-tuple-element.48), custom_call_target="InvertDiagBlocksLowerTriangular" | custom-call | tf_op jit(solution)/shard_map/jit(cholesky)/cholesky | solution.py:131
  445.5 12.0 %cholesky.314 = f32[128,128]{1,0:T(8,128)S(1)} custom-call(f32[128,128]{1,0:T(8,128)S(1)} %cholesky.360), custom_call_target="Cholesky" | custom-call | tf_op jit(solution)/shard_map/jit(cholesky)/cholesky | solution.py:131
  458.2 9.8 %custom-call.42 = f32[1,128,128]{1,2,0:T(8,128)S(1)} custom-call(f32[1,128,128]{2,1,0:T(8,128)S(1)} %get-tuple-element.45), custom_call_target="InvertDiagBlocksLowerTriangular" | custom-call | tf_op jit(solution)/shard_map/jit(cholesky)/cholesky | solution.py:131
  469.0 1.5 cholesky.334
  475.8 12.1 %while.1 = (s32[]{:T(128)}, f32[528,528]{1,0:T(8,128)}, s32[4,2]{0,1:T(2,128)S(1)}, f32[4,128,128]{2,1,0:T(8,128)S(1)}, s32[]{:T(128)}) while((s32[]{:T(128)}, f32[528,528]{1,0:T(8,128)}, s32[4,2]{0,1:T(2,128)S(1)}, f32[4,128,128]{2,1,0:T(8,128)S(1)}, s32[]{:T(128)}) %tuple.74), condition=%wide.while_cond, body=%wide.while_body.sunk | while | flops 2 | bytes 131181 | solution.py:133
  476.5 2.3 bitcast_dynamic-update-slice_fusion.9
  479.5 2.3 bitcast_dynamic-update-slice_fusion.9
  482.5 2.3 bitcast_dynamic-update-slice_fusion.9
  485.6 2.3 bitcast_dynamic-update-slice_fusion.9
  488.0 49.1 %custom-call.43 = f32[5,128,128]{1,2,0:T(8,128)S(1)} custom-call(f32[5,128,128]{2,1,0:T(8,128)S(1)} %pad_maximum_fusion), custom_call_target="InvertDiagBlocksLowerTriangular" | custom-call | tf_op jit(solution)/shard_map/jit(_solve_triangular)/triangular_solve | solution.py:133
  (285 shorter events, 72.4 us)
Async XLA Ops:
  7.2 8.4 %copy-start.3 = (bf16[2,8,16,3072]{3,2,1,0:T(8,128)(2,1)S(1)}, bf16[2,8,16,3072]{3,2,1,0:T(8,128)(2,1)}, u32[]{:S(2)}) copy-start(bf16[2,8,16,3072]{3,2,1,0:T(8,128)(2,1)} %param.8) | copy-start | bytes 4718596
  7.2 201.9 %all-reduce.8.cloned.1.call-start = ((), (), s32[]{:S(2)}) async-start(), calls=%async_computation | async-start | bytes 3932160 | tf_op jit(solution)/shard_map/psum | solution.py:207
  10.0 78.6 %collective-permute-start = (bf16[1,8,16,3072]{3,2,1,0:T(8,128)(2,1)}, bf16[1,8,16,3072]{3,2,1,0:T(8,128)(2,1)}, u32[]{:S(2)}, u32[]{:S(2)}) collective-permute-start(bf16[1,8,16,3072]{3,2,1,0:T(8,128)(2,1)} %get-tuple-element.43), channel_id=1, source_target_pairs={{0,32},{32,64},{64,96},{96,128},{128,160},{160,192},{192,224},{1,3... | collective-permute-start | bytes 2359304 | tf_op jit(solution)/shard_map/ppermute | solution.py:19
  11.9 87.4 %collective-permute-start.1 = (bf16[1,8,16,3072]{3,2,1,0:T(8,128)(2,1)}, bf16[1,8,16,3072]{3,2,1,0:T(8,128)(2,1)}, u32[]{:S(2)}, u32[]{:S(2)}) collective-permute-start(bf16[1,8,16,3072]{3,2,1,0:T(8,128)(2,1)} %get-tuple-element.42), channel_id=1, source_target_pairs={{32,0},{64,32},{96,64},{128,96},{160,128},{192,160},{224,192},{33,... | collective-permute-start | bytes 2359304 | tf_op jit(solution)/shard_map/ppermute | solution.py:20
  26.1 4.1 copy-start.39
  30.3 5.4 copy-start.35
  30.3 5.3 copy-start.43
  30.3 5.6 %copy-start.40 = (f32[2,8,16]{2,1,0:T(8,128)S(1)}, f32[2,8,16]{2,1,0:T(8,128)}, u32[]{:S(2)}) copy-start(f32[2,8,16]{2,1,0:T(8,128)} %param.9) | copy-start | bytes 3076
  30.3 5.7 %copy-start.34 = (bf16[3,64,64]{2,1,0:T(8,128)(2,1)S(1)}, bf16[3,64,64]{2,1,0:T(8,128)(2,1)}, u32[]{:S(2)}) copy-start(bf16[3,64,64]{2,1,0:T(8,128)(2,1)} %param.10) | copy-start | bytes 73732
  36.0 5.3 copy-start
  41.3 2.2 copy-start.2
  43.5 7.9 %copy-start.38 = (f32[3,8,16]{2,1,0:T(8,128)S(1)}, f32[3,8,16]{2,1,0:T(8,128)}, u32[]{:S(2)}) copy-start(f32[3,8,16]{2,1,0:T(8,128)} %param.11) | copy-start | bytes 4612
  51.5 2.2 copy-start.12
  63.8 4.1 copy-start.19
  64.2 2.2 copy-start.41
  66.4 4.3 copy-start.54
  66.4 4.3 copy-start.55
  66.4 4.3 copy-start.56
  66.4 4.3 copy-start.57
  66.4 4.3 copy-start.58
  66.4 4.3 copy-start.59
  66.4 4.3 copy-start.44
  66.4 4.6 copy-start.33
  66.4 5.9 %copy-start.17 = (bf16[1,8,16,1,4,4,48]{6,5,4,3,2,1,0:T(4,128)(2,1)S(1)}, bf16[1,8,16,1,4,4,48]{6,5,4,3,2,1,0:T(4,128)(2,1)}, u32[]{:S(2)}) copy-start(bf16[1,8,16,1,4,4,48]{6,5,4,3,2,1,0:T(4,128)(2,1)} %get-tuple-element.36) | copy-start | bytes 589828
  66.5 5.9 %copy-start.18 = (bf16[1,8,16,1,4,4,48]{6,5,4,3,2,1,0:T(4,128)(2,1)S(1)}, bf16[1,8,16,1,4,4,48]{6,5,4,3,2,1,0:T(4,128)(2,1)}, u32[]{:S(2)}) copy-start(bf16[1,8,16,1,4,4,48]{6,5,4,3,2,1,0:T(4,128)(2,1)} %get-tuple-element.37) | copy-start | bytes 589828
  66.6 2.3 copy-start.30
  67.2 3.5 copy-start.45
  68.9 5.4 copy-start.15
  68.9 5.7 %copy-start.21 = (bf16[7,2,16,16,48]{4,2,3,0,1:T(8,128)(2,1)S(1)}, bf16[7,2,16,16,48]{4,2,3,0,1:T(8,128)(2,1)}, u32[]{:S(2)}) copy-start(bf16[7,2,16,16,48]{4,2,3,0,1:T(8,128)(2,1)} %multiply_convert_fusion.3) | copy-start | bytes 1032196
  71.1 2.9 copy-start.50
  72.4 3.4 copy-start.1
  78.4 2.9 copy-start.8
  109.7 8.3 %copy-start.20 = (f32[1,8,16,1,4,4,48]{6,1,5,4,2,3,0:T(8,128)S(1)}, f32[1,8,16,1,4,4,48]{6,1,5,4,2,3,0:T(8,128)}, u32[]{:S(2)}) copy-start(f32[1,8,16,1,4,4,48]{6,1,5,4,2,3,0:T(8,128)} %copy.245) | copy-start | bytes 1179652
  109.7 8.3 %copy-start.42 = (f32[1,8,16]{1,2,0:T(8,128)S(1)}, f32[1,8,16]{1,2,0:T(8,128)}, u32[]{:S(2)}) copy-start(f32[1,8,16]{1,2,0:T(8,128)} %get-tuple-element.55) | copy-start | bytes 1540
  112.0 6.5 %copy-start.25 = (f32[4,48,48]{2,1,0:T(8,128)S(1)}, f32[4,48,48]{2,1,0:T(8,128)}, u32[]{:S(2)}) copy-start(f32[4,48,48]{2,1,0:T(8,128)} %convolution_bitcast_fusion.12) | copy-start | bytes 110596
  112.0 6.5 %copy-start.26 = (f32[4,48,48]{2,1,0:T(8,128)S(1)}, f32[4,48,48]{2,1,0:T(8,128)}, u32[]{:S(2)}) copy-start(f32[4,48,48]{2,1,0:T(8,128)} %convolution_bitcast_fusion.13) | copy-start | bytes 110596
  112.0 6.5 %copy-start.32 = (f32[4,48,48]{2,1,0:T(8,128)S(1)}, f32[4,48,48]{2,1,0:T(8,128)}, u32[]{:S(2)}) copy-start(f32[4,48,48]{2,1,0:T(8,128)} %fusion.24) | copy-start | bytes 110596
  112.0 12.5 %collective-permute-start.2 = (bf16[4,1,16,3072]{3,2,1,0:T(8,128)(2,1)}, bf16[4,1,16,3072]{3,2,1,0:T(8,128)(2,1)}, u32[]{:S(2)}, u32[]{:S(2)}) collective-permute-start(bf16[4,1,16,3072]{3,2,1,0:T(8,128)(2,1)} %get-tuple-element.41), channel_id=1, source_target_pairs={{0,1},{1,2},{2,3},{3,4},{4,5},{5,6},{6,7},{7,8},{8,9},{9,10},{10,1... | collective-permute-start | bytes 1179656 | tf_op jit(solution)/shard_map/ppermute | solution.py:19
  116.7 12.6 %collective-permute-start.3 = (bf16[4,1,16,3072]{3,2,1,0:T(8,128)(2,1)}, bf16[4,1,16,3072]{3,2,1,0:T(8,128)(2,1)}, u32[]{:S(2)}, u32[]{:S(2)}) collective-permute-start(bf16[4,1,16,3072]{3,2,1,0:T(8,128)(2,1)} %get-tuple-element.40), channel_id=1, source_target_pairs={{1,0},{2,1},{3,2},{4,3},{5,4},{6,5},{7,6},{8,7},{9,8},{10,9},{11,1... | collective-permute-start | bytes 1179656 | tf_op jit(solution)/shard_map/ppermute | solution.py:20
  121.8 9.0 %copy-start.16 = (f32[1,2,16,16,48]{4,2,3,0,1:T(8,128)S(1)}, f32[1,2,16,16,48]{4,2,3,0,1:T(8,128)}, u32[]{:S(2)}) copy-start(f32[1,2,16,16,48]{4,2,3,0,1:T(8,128)} %slice_convert_fusion.1) | copy-start | bytes 294916
  125.9 5.6 %slice-start = ((bf16[2,8,4,16,48]{4,1,3,2,0:T(8,128)(2,1)}), bf16[2,8,3,16,48]{4,1,3,2,0:T(8,128)(2,1)S(1)}, s32[]{:S(2)}) async-start(bf16[2,8,4,16,48]{4,1,3,2,0:T(8,128)(2,1)} %slice_bitcast_fusion), calls=%async_computation.2 | async-start | bytes 393216 | tf_op jit(solution)/shard_map/slice | solution.py:87
  126.0 5.6 %copy-start.48 = (f32[2,8,4]{1,2,0:T(4,128)S(1)}, f32[2,8,4]{1,2,0:T(4,128)}, u32[]{:S(2)}) copy-start(f32[2,8,4]{1,2,0:T(4,128)} %get-tuple-element.66) | copy-start | bytes 772
  130.8 2.0 slice-start.1
  131.5 3.3 copy-start.49
  139.0 227.6 %all-reduce.10.cloned.1.call-start = ((), (), s32[]{:S(2)}) async-start(), calls=%async_computation.1 | async-start | bytes 2703360 | tf_op jit(solution)/shard_map/psum | solution.py:207
  366.6 3.0 copy-start.7
  474.5 13.4 %copy-start.28 = (f32[128,112]{1,0:T(8,128)S(1)}, f32[128,112]{1,0:T(8,128)}, u32[]{:S(2)}) copy-start(f32[128,112]{1,0:T(8,128)} %pad_convert_fusion) | copy-start | bytes 172036
  538.5 4.8 copy-start.60
  (26 other events, 36.0 us)
Sparse Core Ops, SparseCore 0:
  139.1 69.9 all-reduce.7
  212.8 153.7 all-reduce.9
